TPU v7x, 32 devices: a whole 2x2x4 slice. The times are simulated.
32 devices in a mesh: dp: 4 (over y, core), fsdp: 8 (over z, x).
Axes of the slice: x: 2, y: 2, z: 4, core: 2. Of those that a mesh axis runs over, the one named last changes fastest.
Arguments:
- hidden_in: bfloat16 [20480, 768], P(('dp', 'fsdp')), may hold values from -7 to 7
- prev_logits: bfloat16 [32, 12, 640, 640], P(('dp', 'fsdp')), may hold values from -6 to 6
- segment_ids: int32 [32, 640], P(('dp', 'fsdp')), may hold values from 0 to 3, never falling along the last dimension, each value on 1 to 320 neighbouring positions
- d_hidden: bfloat16 [20480, 768], P(('dp', 'fsdp')), may hold values from -6 to 6
- d_logits: bfloat16 [32, 12, 640, 640], P(('dp', 'fsdp')), may hold values from -3 to 3
- weight_in: float32 [768, 5376], P(('dp', 'fsdp')), may hold values from -2.5 to 2.5
- weight_out: float32 [3840, 768], P(('dp', 'fsdp')), may hold values from -2 to 2
- vectors: float32 [12, 768], P(None, ('dp', 'fsdp')), may hold values from -0.6 to 1.45
- moment_in: float32 [768, 5376], P(('dp', 'fsdp')), may hold values from -0.55 to 0.55
- moment_out: float32 [3840, 768], P(('dp', 'fsdp')), may hold values from -0.55 to 0.55
- moment_vectors: float32 [12, 768], P(None, ('dp', 'fsdp')), may hold values from -1.5 to 1.5
- square_in: float32 [768, 5376], P(('dp', 'fsdp')), may hold values from 0.001 to 0.004
- square_out: float32 [3840, 768], P(('dp', 'fsdp')), may hold values from 0.001 to 0.004
- square_vectors: float32 [12, 768], P(None, ('dp', 'fsdp')), may hold values from 0.008 to 0.032
- step_count: int32 [1], replicated, may hold values from 1 to 20
Outputs:
- hidden_out: bfloat16 [20480, 768], P(('dp', 'fsdp'))
- logits: bfloat16 [32, 12, 640, 640], P(('dp', 'fsdp'))
- d_input: bfloat16 [20480, 768], P(('dp', 'fsdp'))
- d_prev: bfloat16 [32, 12, 640, 640], P(('dp', 'fsdp'))
- grad_weight_in: float32 [768, 5376], P(('dp', 'fsdp'))
- grad_weight_out: float32 [3840, 768], P(('dp', 'fsdp'))
- grad_vectors: float32 [12, 768], P(None, ('dp', 'fsdp'))
- new_moment_in: float32 [768, 5376], P(('dp', 'fsdp'))
- new_moment_out: float32 [3840, 768], P(('dp', 'fsdp'))
- new_moment_vectors: float32 [12, 768], P(None, ('dp', 'fsdp'))
- new_square_in: float32 [768, 5376], P(('dp', 'fsdp'))
- new_square_out: float32 [3840, 768], P(('dp', 'fsdp'))
- new_square_vectors: float32 [12, 768], P(None, ('dp', 'fsdp'))
- new_weight_in: float32 [768, 5376], P(('dp', 'fsdp'))
- new_weight_out: float32 [3840, 768], P(('dp', 'fsdp'))
- new_vectors: float32 [12, 768], P(None, ('dp', 'fsdp'))
- copy_weight_in: bfloat16 [768, 5376], P(('dp', 'fsdp'))
- copy_weight_out: bfloat16 [3840, 768], P(('dp', 'fsdp'))
- copy_vectors: bfloat16 [12, 768], P(None, ('dp', 'fsdp'))
- grad_norm: float32 [], replicated
Inputs may be any that keep to these rules, and one draw needn't show every extreme that they name: `segment_ids`: along each row the segment numbers never fall; no segment holds more than 320 slots.
All inputs are finite; a program needn't handle non-finite values.
Results may differ from a plain program's by a relative error of at most 0.012.
Values may be sent and summed in bfloat16 or wider, within the bound.
A program may use at most 192 MiB of HBM per device.

v0:
```python
import math
import jax
import jax.numpy as jnp
from jax import lax
from jax.sharding import PartitionSpec as P

PARAMS = 7087104
norm_eps = 1e-12
clip_scale = 1.0
beta_one = 0.9
beta_two = 0.999
adam_eps = 1e-08
rate_matrix = 0.06
rate_vector = 0.25
decay_matrix = 0.01
masked_fill = -1e30


def gelu_exact(upward):
    return jax.nn.gelu(upward, approximate=False)


def norm_rows(residual, gain_row, shift_row):
    centered = residual - jnp.mean(residual, axis=1, keepdims=True)
    scaling = lax.rsqrt(jnp.mean(centered * centered, axis=1, keepdims=True) + norm_eps)
    normed = centered * scaling
    return (normed * gain_row + shift_row, normed, scaling)


def norm_back(grad_after, normed, scaling, gain_row):
    scaled_grad = grad_after * gain_row
    return scaling * (
        scaled_grad
        - jnp.mean(scaled_grad, axis=1, keepdims=True)
        - normed * jnp.mean(scaled_grad * normed, axis=1, keepdims=True)
    )


def split_heads(matrix, head_count):
    return matrix.reshape(matrix.shape[0], head_count, -1)


def forward(weights, tokens, previous, same_doc):
    weight_in, weight_out, vectors = weights
    model_width = weight_out.shape[1]
    head_count = previous.shape[0]
    row_count = tokens.shape[0]
    score_scale = (model_width // head_count) ** (-0.5)
    vector_rows = vectors.astype(jnp.float32)
    projected = jnp.dot(tokens, weight_in[:, : 3 * model_width], preferred_element_type=jnp.float32)
    queries = (projected[:, :model_width] + vector_rows[4]).astype(jnp.bfloat16)
    keys_low = projected[:, model_width : 2 * model_width].astype(jnp.bfloat16)
    values_low = (projected[:, 2 * model_width :] + vector_rows[5]).astype(jnp.bfloat16)
    scores = jnp.einsum(
        "qhd,khd->hqk",
        split_heads(queries, head_count),
        split_heads(keys_low, head_count),
        preferred_element_type=jnp.float32,
    ) * score_scale + previous.astype(jnp.float32)
    masked = jnp.where(same_doc[None], scores, masked_fill)
    row_max = jnp.max(masked, axis=2, keepdims=True)
    expo_terms = jnp.exp(masked - row_max)
    totals = jnp.sum(expo_terms, axis=2, keepdims=True)
    attn_probs = expo_terms / totals
    log_sums = row_max + jnp.log(totals)
    mixed_heads = jnp.einsum(
        "hqk,khd->qhd",
        attn_probs.astype(jnp.bfloat16),
        split_heads(values_low, head_count),
        preferred_element_type=jnp.float32,
    )
    mixed_heads = mixed_heads.reshape(row_count, model_width).astype(jnp.bfloat16)
    first_sum = tokens.astype(jnp.float32) + (
        jnp.dot(mixed_heads, weight_out[:model_width], preferred_element_type=jnp.float32)
        + vector_rows[6]
    )
    hidden_one, normed_one, scale_one = norm_rows(first_sum, vector_rows[0], vector_rows[2])
    hidden_low = hidden_one.astype(jnp.bfloat16)
    upward = jnp.dot(
        hidden_low, weight_in[:, 3 * model_width :], preferred_element_type=jnp.float32
    ) + vector_rows[8:].reshape(-1)
    activated = gelu_exact(upward).astype(jnp.bfloat16)
    second_sum = hidden_one + (
        jnp.dot(activated, weight_out[model_width:], preferred_element_type=jnp.float32)
        + vector_rows[7]
    )
    output, normed_two, scale_two = norm_rows(second_sum, vector_rows[1], vector_rows[3])
    kept_values = (
        queries,
        keys_low,
        values_low,
        log_sums,
        mixed_heads,
        normed_one,
        scale_one,
        hidden_low,
        upward,
        activated,
        normed_two,
        scale_two,
    )
    return (output, scores, kept_values)


def backward(weights, kept_values, tokens, previous, same_doc, grad_hidden, grad_logits):
    weight_in, weight_out, vectors = weights
    (
        queries,
        keys_low,
        values_low,
        log_sums,
        mixed_heads,
        normed_one,
        scale_one,
        hidden_low,
        upward,
        activated,
        normed_two,
        scale_two,
    ) = kept_values
    model_width = weight_out.shape[1]
    head_count = previous.shape[0]
    row_count = tokens.shape[0]
    score_scale = (model_width // head_count) ** (-0.5)
    vector_rows = vectors.astype(jnp.float32)
    grad_output = grad_hidden.astype(jnp.float32)
    gain_two_grad = jnp.sum(grad_output * normed_two, axis=0)
    shift_two_grad = jnp.sum(grad_output, axis=0)
    grad_second = norm_back(grad_output, normed_two, scale_two, vector_rows[1])
    grad_down = grad_second.astype(jnp.bfloat16)
    bias_down_grad = jnp.sum(grad_down, axis=0, dtype=jnp.float32)
    down_grad = jnp.einsum("tf,td->fd", activated, grad_down, preferred_element_type=jnp.float32)
    grad_activated = jnp.einsum(
        "td,fd->tf", grad_down, weight_out[model_width:], preferred_element_type=jnp.float32
    )
    unused_value, gelu_pull = jax.vjp(gelu_exact, upward)
    grad_up = gelu_pull(grad_activated)[0].astype(jnp.bfloat16)
    bias_up_grad = jnp.sum(grad_up, axis=0, dtype=jnp.float32)
    up_grad = jnp.einsum("td,tf->df", hidden_low, grad_up, preferred_element_type=jnp.float32)
    grad_hidden_one = grad_second + jnp.einsum(
        "tf,df->td", grad_up, weight_in[:, 3 * model_width :], preferred_element_type=jnp.float32
    )
    gain_one_grad = jnp.sum(grad_hidden_one * normed_one, axis=0)
    shift_one_grad = jnp.sum(grad_hidden_one, axis=0)
    grad_first = norm_back(grad_hidden_one, normed_one, scale_one, vector_rows[0])
    grad_attn = grad_first.astype(jnp.bfloat16)
    bias_out_grad = jnp.sum(grad_attn, axis=0, dtype=jnp.float32)
    attn_grad = jnp.einsum("tc,td->cd", mixed_heads, grad_attn, preferred_element_type=jnp.float32)
    grad_mixed = jnp.einsum(
        "td,cd->tc", grad_attn, weight_out[:model_width], preferred_element_type=jnp.float32
    ).astype(jnp.bfloat16)
    head_queries = split_heads(queries, head_count)
    head_keys = split_heads(keys_low, head_count)
    head_values = split_heads(values_low, head_count)
    head_grad_mixed = split_heads(grad_mixed, head_count)
    scores = jnp.einsum(
        "qhd,khd->hqk", head_queries, head_keys, preferred_element_type=jnp.float32
    ) * score_scale + previous.astype(jnp.float32)
    attn_probs = jnp.exp(jnp.where(same_doc[None], scores, masked_fill) - log_sums)
    grad_probs = jnp.einsum(
        "qhd,khd->hqk", head_grad_mixed, head_values, preferred_element_type=jnp.float32
    )
    grad_scores = attn_probs * (
        grad_probs - jnp.sum(attn_probs * grad_probs, axis=2, keepdims=True)
    )
    grad_total = (grad_scores + grad_logits.astype(jnp.float32)).astype(jnp.bfloat16)
    grad_queries = (
        (
            jnp.einsum("hqk,khd->qhd", grad_total, head_keys, preferred_element_type=jnp.float32)
            * score_scale
        )
        .astype(jnp.bfloat16)
        .reshape(row_count, model_width)
    )
    grad_keys = (
        (
            jnp.einsum("hqk,qhd->khd", grad_total, head_queries, preferred_element_type=jnp.float32)
            * score_scale
        )
        .astype(jnp.bfloat16)
        .reshape(row_count, model_width)
    )
    grad_values = (
        jnp.einsum(
            "hqk,qhd->khd",
            attn_probs.astype(jnp.bfloat16),
            head_grad_mixed,
            preferred_element_type=jnp.float32,
        )
        .astype(jnp.bfloat16)
        .reshape(row_count, model_width)
    )
    grad_projected = jnp.concatenate([grad_queries, grad_keys, grad_values], axis=1)
    qkv_grad = jnp.einsum("td,tc->dc", tokens, grad_projected, preferred_element_type=jnp.float32)
    grad_tokens = grad_first + jnp.einsum(
        "tc,dc->td",
        grad_projected,
        weight_in[:, : 3 * model_width],
        preferred_element_type=jnp.float32,
    )
    small_rows = jnp.stack(
        [
            gain_one_grad,
            gain_two_grad,
            shift_one_grad,
            shift_two_grad,
            jnp.sum(grad_queries, axis=0, dtype=jnp.float32),
            jnp.sum(grad_values, axis=0, dtype=jnp.float32),
            bias_out_grad,
            bias_down_grad,
        ]
    )
    small_grads = jnp.concatenate([small_rows, bias_up_grad.reshape(-1, model_width)], axis=0)
    return (
        jnp.concatenate([qkv_grad, up_grad], axis=1),
        jnp.concatenate([attn_grad, down_grad], axis=0),
        small_grads,
        grad_tokens.astype(jnp.bfloat16),
        grad_total,
    )


def adam_update(master, moment, square, gradient, factor, step_value, step_rate, decay_rate):
    clipped = gradient * factor
    new_moment = beta_one * moment + (1.0 - beta_one) * clipped
    new_square = beta_two * square + (1.0 - beta_two) * clipped * clipped
    fixed_moment = new_moment / (1.0 - jnp.power(beta_one, step_value))
    fixed_square = new_square / (1.0 - jnp.power(beta_two, step_value))
    updated = master - step_rate * (
        fixed_moment / (jnp.sqrt(fixed_square) + adam_eps) + decay_rate * master
    )
    return (clipped, new_moment, new_square, updated)


def body(
    hidden_in,
    prev_logits,
    segment_ids,
    d_hidden,
    d_logits,
    weight_in,
    weight_out,
    vectors,
    moment_in,
    moment_out,
    moment_vectors,
    square_in,
    square_out,
    square_vectors,
    step_count,
):
    low_in = weight_in.astype(jnp.bfloat16)
    low_out = weight_out.astype(jnp.bfloat16)
    low_small = vectors.astype(jnp.bfloat16)
    gathered = (
        lax.all_gather(low_in, ("dp", "fsdp"), axis=0, tiled=True),
        lax.all_gather(low_out, ("dp", "fsdp"), axis=0, tiled=True),
        lax.all_gather(low_small, ("dp", "fsdp"), axis=1, tiled=True),
    )
    segments = segment_ids[0]
    same_doc = segments[:, None] == segments[None, :]
    previous = prev_logits[0]
    output, scores, kept_values = forward(gathered, hidden_in, previous, same_doc)
    regathered = (
        lax.all_gather(low_in, ("dp", "fsdp"), axis=0, tiled=True),
        lax.all_gather(low_out, ("dp", "fsdp"), axis=0, tiled=True),
        lax.all_gather(low_small, ("dp", "fsdp"), axis=1, tiled=True),
    )
    unused_out, unused_scores, again_values = forward(regathered, hidden_in, previous, same_doc)
    full_in, full_out, full_small, grad_tokens, grad_prev = backward(
        regathered, again_values, hidden_in, previous, same_doc, d_hidden, d_logits[0]
    )
    owned_in, owned_out, owned_small = (
        lax.psum_scatter(full_in, ("dp", "fsdp"), scatter_dimension=0, tiled=True),
        lax.psum_scatter(full_out, ("dp", "fsdp"), scatter_dimension=0, tiled=True),
        lax.psum_scatter(full_small, ("dp", "fsdp"), scatter_dimension=1, tiled=True),
    )
    local_squares = (
        jnp.sum(owned_in * owned_in)
        + jnp.sum(owned_out * owned_out)
        + jnp.sum(owned_small * owned_small)
    )
    total_squares = lax.psum(local_squares, ("dp", "fsdp"))
    grad_norm = jnp.sqrt(total_squares)
    threshold = clip_scale * math.sqrt(PARAMS)
    factor = jnp.minimum(1.0, threshold / (grad_norm + 1e-06))
    step_value = step_count[0].astype(jnp.float32)
    clip_in, moment_one, square_one, updated_in = adam_update(
        weight_in, moment_in, square_in, owned_in, factor, step_value, rate_matrix, decay_matrix
    )
    clip_out, moment_two, square_two, updated_out = adam_update(
        weight_out, moment_out, square_out, owned_out, factor, step_value, rate_matrix, decay_matrix
    )
    clip_small, moment_three, square_three, updated_small = adam_update(
        vectors, moment_vectors, square_vectors, owned_small, factor, step_value, rate_vector, 0.0
    )
    return (
        output.astype(jnp.bfloat16),
        scores.astype(jnp.bfloat16)[None],
        grad_tokens,
        grad_prev[None],
        clip_in,
        clip_out,
        clip_small,
        moment_one,
        moment_two,
        moment_three,
        square_one,
        square_two,
        square_three,
        updated_in,
        updated_out,
        updated_small,
        updated_in.astype(jnp.bfloat16),
        updated_out.astype(jnp.bfloat16),
        updated_small.astype(jnp.bfloat16),
        grad_norm,
    )


def solution(mesh):
    return jax.shard_map(
        body,
        mesh=mesh,
        in_specs=(
            P(("dp", "fsdp"), None),
            P(("dp", "fsdp"), None, None, None),
            P(("dp", "fsdp"), None),
            P(("dp", "fsdp"), None),
            P(("dp", "fsdp"), None, None, None),
            P(("dp", "fsdp"), None),
            P(("dp", "fsdp"), None),
            P(None, ("dp", "fsdp")),
            P(("dp", "fsdp"), None),
            P(("dp", "fsdp"), None),
            P(None, ("dp", "fsdp")),
            P(("dp", "fsdp"), None),
            P(("dp", "fsdp"), None),
            P(None, ("dp", "fsdp")),
            P(),
        ),
        out_specs=(
            P(("dp", "fsdp"), None),
            P(("dp", "fsdp"), None, None, None),
            P(("dp", "fsdp"), None),
            P(("dp", "fsdp"), None, None, None),
            P(("dp", "fsdp"), None),
            P(("dp", "fsdp"), None),
            P(None, ("dp", "fsdp")),
            P(("dp", "fsdp"), None),
            P(("dp", "fsdp"), None),
            P(None, ("dp", "fsdp")),
            P(("dp", "fsdp"), None),
            P(("dp", "fsdp"), None),
            P(None, ("dp", "fsdp")),
            P(("dp", "fsdp"), None),
            P(("dp", "fsdp"), None),
            P(None, ("dp", "fsdp")),
            P(("dp", "fsdp"), None),
            P(("dp", "fsdp"), None),
            P(None, ("dp", "fsdp")),
            P(),
        ),
        check_vma=False,
    )
```

profile of v0, /device:TPU:0, one launch (start us, length us, event | category | flops | bytes accessed | tf_op | source)
XLA Modules:
  0.0 645.5 jit_solution(6729992086085996024)
XLA Ops:
  11.5 71.6 %all-gather = bf16[32,24,12]{1,2,0:T(8,128)(2,1)S(1)} all-gather(bf16[1,24,12]{1,2,0:T(8,128)(2,1)S(1)} %convert_bitcast_fusion.1), channel_id=1, replica_groups=mesh['dp'=4,'fsdp'=8] {'dp','fsdp'}, dimensions={0}, use_global_device_ids=true | all-gather | bytes 19008 | tf_op jit(solution)/shard_map/all_gather | solution.py:258
  83.5 14.0 %copy.85 = bf16[1,12,640,640]{2,3,1,0:T(8,128)(2,1)} copy(bf16[1,12,640,640]{3,2,1,0:T(8,128)(2,1)} %param.16) | data formatting | bytes 19660800 | tf_op args[1]
  107.1 11.9 %select_reduce_fusion = (f32[12,640]{1,0:T(8,128)S(1)}, f32[12,640,640]{1,2,0:T(8,128)}) fusion(pred[640,640]{0,1:T(8,128)(4,1)S(1)} %broadcast_compare_fusion, bf16[1,12,640,640]{2,3,1,0:T(8,128)(2,1)} %copy.85, bf16[640,12,64]{0,2,1:T(8,128)(2,1)S(1)} %bitcast.63, bf16[640,12,64]{0,2,1:T(8,128)(2,1)S(1)} %bitcast.61), kind=kOutput, calls=%fused_computation.11 | convolution fusion | flops 653713920 | bytes 31897600 | tf_op jit(solution)/shard_map/qhd,khd->hqk/dot_general | solution.py:54
  119.0 17.7 %convert_bitcast_fusion = (bf16[1,12,640,640]{2,3,1,0:T(8,128)(2,1)}, f32[12,640]{1,0:T(8,128)S(1)}) fusion(f32[12,640,640]{1,2,0:T(8,128)} %get-tuple-element.143, f32[12,640]{1,0:T(8,128)S(1)} %get-tuple-element.142, pred[640,640]{0,1:T(8,128)(4,1)S(1)} %broadcast_compare_fusion), kind=kLoop, calls=%fused_computation.18 | loop fusion | flops 19653120 | bytes 29962240 | tf_op jit(solution)/shard_map/broadcast_in_dim | solution.py:299
  136.8 10.8 %fusion.55 = bf16[12,64,640]{2,1,0:T(8,128)(2,1)} fusion(bf16[640,12,64]{0,2,1:T(8,128)(2,1)S(1)} %bitcast.67, f32[12,640,640]{1,2,0:T(8,128)} %get-tuple-element.143, f32[12,640]{1,0:T(8,128)S(1)} %get-tuple-element.138, f32[12,640]{1,0:T(8,128)S(1)} %get-tuple-element.142, pred[640,640]{0,1:T(8,128)(4,1)S(1)} %broadcast_compare_fusion), kind=kOutput, calls=%fused_computation.92 | convolution fusion | flops 649297920 | bytes 22097920 | tf_op jit(solution)/shard_map/hqk,khd->qhd/dot_general | solution.py:66
  147.6 14.3 %all-gather.6.cloned.1.call-done = bf16[3840,768]{1,0:T(8,128)(2,1)} async-done(((bf16[120,768]{1,0:T(8,128)(2,1)}), bf16[3840,768]{1,0:T(8,128)(2,1)}) %all-gather.6.cloned.1.call-update) | async-done | bytes 5898256 | tf_op jit(solution)/shard_map/all_gather | solution.py:257
  165.4 23.9 %multiply_convert_fusion = (bf16[640,3072]{1,0:T(8,128)(2,1)S(1)}, f32[640,3072]{1,0:T(8,128)}, f32[640,3072]{1,0:T(8,128)}) fusion(f32[3072]{0:T(1024)S(1)} %add.219, bf16[768,5376]{1,0:T(8,128)(2,1)} %all-gather.4.cloned.1.call-done, f32[640,768]{1,0:T(8,128)S(1)} %get-tuple-element.145, f32[768]{0:T(1024)S(1)} %get-tuple-element.111, ...), kind=kOutput, calls=%fused_computation.27 | convolution fusion | flops 3152117760 | bytes 26369024 | tf_op jit(solution)/shard_map/dot_general | solution.py:79
  195.9 6.4 fusion.69
  202.3 10.9 %convert_reduce_fusion = (f32[3072]{0:T(1024)S(1)}, bf16[640,3072]{1,0:T(8,128)(2,1)S(1)}) fusion(f32[640,3072]{1,0:T(8,128)} %get-tuple-element.136, bf16[3840,768]{1,0:T(8,128)(2,1)} %all-gather.6.cloned.1.call-done, f32[640,768]{1,0:T(8,128)S(1)} %get-tuple-element.132, f32[640,3072]{1,0:T(8,128)} %get-tuple-element.146, f32[3072]{0:T(1024)S(1)} %add.219), kind=kOutput, calls=%fused_computation.25 | convolution fusion | flops 3053810688 | bytes 26370048 | tf_op jit(solution)/shard_map/td,fd->tf/dot_general | solution.py:133
  221.5 9.5 %pad_maximum_fusion.1 = f32[3840,768]{1,0:T(8,128)} fusion(f32[3072,768]{1,0:T(8,128)} %fusion.69, f32[768,768]{1,0:T(8,128)} %fusion.66), kind=kLoop, calls=%fused_computation.13 | loop fusion | flops 2949120 | bytes 23592960 | tf_op jit(solution)/shard_map/concatenate | solution.py:216
  231.1 15.4 %copy.88 = bf16[1,12,640,640]{2,3,1,0:T(8,128)(2,1)} copy(bf16[1,12,640,640]{3,2,1,0:T(8,128)(2,1)} %param.19) | data formatting | bytes 19660800 | tf_op args[4]
  250.9 28.2 %fusion.1 = bf16[12,640,640]{1,2,0:T(8,128)(2,1)} fusion(f32[12,640,640]{1,2,0:T(8,128)} %get-tuple-element.143, bf16[1,12,640,640]{2,3,1,0:T(8,128)(2,1)} %copy.88, f32[12,640]{1,0:T(8,128)S(1)} %log_add_fusion, pred[640,640]{0,1:T(8,128)(4,1)S(1)} %broadcast_compare_fusion, bf16[640,12,64]{0,2,1:T(8,128)(2,1)} %bitcast.73, bf16[640,12,64]{0,2,1:T(8,128)(2,1)} %bitcast.68), kind=kOutput, calls=%fused_computation.2 | convolution fusion | flops 1307451520 | bytes 41728000 | tf_op jit(solution)/shard_map/sub | solution.py:164
  279.2 5.8 convert_reduce_fusion.5
  290.2 11.5 %convert_reduce_fusion.4 = (f32[12,64]{1,0:T(8,128)S(1)}, bf16[12,64,640]{2,1,0:T(8,128)(2,1)S(1)}) fusion(bf16[640,12,64]{0,2,1:T(8,128)(2,1)S(1)} %bitcast.74, f32[12,640,640]{1,2,0:T(8,128)} %get-tuple-element.143, f32[12,640]{1,0:T(8,128)S(1)} %log_add_fusion, pred[640,640]{0,1:T(8,128)(4,1)S(1)} %broadcast_compare_fusion), kind=kOutput, calls=%fused_computation.73 | convolution fusion | flops 645364992 | bytes 22070272 | tf_op jit(solution)/shard_map/hqk,qhd->khd/dot_general | solution.py:184
  302.8 7.9 %convolution_bitcast_fusion = f32[768,2304]{0,1:T(8,128)} fusion(bf16[640,768]{1,0:T(8,128)(2,1)S(1)} %copy-done.29, bf16[640,768]{0,1:T(8,128)(2,1)S(1)} %bitcast.81, bf16[640,768]{0,1:T(8,128)(2,1)S(1)} %bitcast.69, bf16[640,768]{0,1:T(8,128)(2,1)S(1)} %bitcast.65), kind=kOutput, calls=%fused_computation.41 | convolution fusion | flops 2273771520 | bytes 11010048 | tf_op jit(solution)/shard_map/td,tc->dc/dot_general | solution.py:194
  310.7 8.2 %copy.92 = f32[768,2304]{1,0:T(8,128)} copy(f32[768,2304]{0,1:T(8,128)} %convolution_bitcast_fusion) | data formatting | bytes 14155776 | tf_op jit(solution)/shard_map/td,tc->dc/dot_general | solution.py:194
  318.9 6.6 %fusion.75 = f32[768,3072]{1,0:T(8,128)S(1)} fusion(bf16[640,3072]{1,0:T(8,128)(2,1)} %copy-done.9, f32[640,768]{1,0:T(8,128)S(1)} %get-tuple-element.145, f32[768]{0:T(1024)S(1)} %get-tuple-element.111, f32[768]{0:T(1024)S(1)} %get-tuple-element.112, f32[640]{0:T(1024)S(1)} %add_rsqrt_fusion.1, f32[640]{0:T(1024)S(1)} %broadcast_multiply_fusion.7), kind=kOutput, calls=%fused_computation.145 | convolution fusion | flops 3022356480 | bytes 15346688 | tf_op jit(solution)/shard_map/td,tf->df/dot_general | solution.py:139
  325.5 6.0 pad_maximum_fusion
  332.5 13.9 %copy.94 = bf16[1,12,640,640]{3,2,1,0:T(8,128)(2,1)} copy(bf16[1,12,640,640]{2,3,1,0:T(8,128)(2,1)} %bitcast.60) | data formatting | bytes 19660800
  346.4 39.7 %all-reduce = f32[12,768]{1,0:T(8,128)S(1)} all-reduce(f32[12,768]{1,0:T(8,128)S(1)} %concatenate.15), channel_id=4, replica_groups=mesh['dp'=4,'fsdp'=8] {'dp','fsdp'}, use_global_device_ids=true, to_apply=%region_24.25.clone | all-reduce | flops 9216 | bytes 73728
  386.9 6.0 add_convert_fusion.1
  394.6 180.7 %reduce-scatter.4.cloned.1.call-done = f32[24,5376]{1,0:T(8,128)} async-done(((f32[768,5376]{1,0:T(8,128)}), f32[24,5376]{1,0:T(8,128)}) %reduce-scatter.4.cloned.1.call-update) | async-done | bytes 516112 | tf_op jit(solution)/shard_map/reduce_scatter | solution.py:274
  579.2 13.9 %copy.93 = bf16[1,12,640,640]{3,2,1,0:T(8,128)(2,1)} copy(bf16[1,12,640,640]{2,3,1,0:T(8,128)(2,1)} %get-tuple-element.137) | data formatting | bytes 19660800
  593.2 39.3 %psum.7 = f32[]{:T(128)} all-reduce(f32[]{:T(128)S(6)} %add.235), channel_id=1, replica_groups=mesh['dp'=4,'fsdp'=8] {'dp','fsdp'}, use_global_device_ids=true, to_apply=%region_26.27 | all-reduce | flops 1 | bytes 8 | tf_op jit(solution)/shard_map/psum | solution.py:283
  (135 shorter events, 51.8 us)
Async XLA Ops:
  7.2 90.8 %all-gather.4.cloned.1.call-start = ((), (), s32[]{:S(2)}) async-start(), calls=%async_computation.2 | async-start | bytes 8515584 | tf_op jit(solution)/shard_map/all_gather | solution.py:256
  9.0 152.9 %all-gather.6.cloned.1.call-start = ((), (), s32[]{:S(2)}) async-start(), calls=%async_computation.3 | async-start | bytes 6082560 | tf_op jit(solution)/shard_map/all_gather | solution.py:257
  10.8 382.1 %reduce-scatter.6.cloned.1.call-start = ((), (), s32[]{:S(2)}) async-start(), calls=%async_computation.5 | async-start | bytes 12165120 | tf_op jit(solution)/shard_map/reduce_scatter | solution.py:275
  83.5 14.4 %copy-start.28 = (bf16[640,768]{1,0:T(8,128)(2,1)S(1)}, bf16[640,768]{1,0:T(8,128)(2,1)}, u32[]{:S(2)}) copy-start(bf16[640,768]{1,0:T(8,128)(2,1)} %param.15) | copy-start | bytes 2949124
  104.5 14.5 %copy-start.4 = (bf16[640,768]{0,1:T(8,128)(2,1)}, bf16[640,768]{0,1:T(8,128)(2,1)S(1)}, u32[]{:S(2)}) copy-start(bf16[640,768]{0,1:T(8,128)(2,1)S(1)} %copy.83) | copy-start | bytes 2949124
  107.1 29.7 %copy-start.16 = (bf16[640,768]{0,1:T(8,128)(2,1)}, bf16[640,768]{0,1:T(8,128)(2,1)S(1)}, u32[]{:S(2)}) copy-start(bf16[640,768]{0,1:T(8,128)(2,1)S(1)} %copy.82) | copy-start | bytes 2949124
  161.9 27.4 %slice-start.2 = ((s8[5898240]{0:T(1024)(128)(4,1)}), s8[4194304]{0:T(1024)(128)(4,1)S(1)}, s32[]{:S(2)}) async-start(s8[5898240]{0:T(1024)(128)(4,1)} %bitcast.79), calls=%async_computation.8 | async-start | bytes 8388608
  165.4 23.9 %slice-start.3 = ((s8[5898240]{0:T(1024)(128)(4,1)}), s8[1703936]{0:T(1024)(128)(4,1)S(1)}, s32[]{:S(2)}) async-start(s8[5898240]{0:T(1024)(128)(4,1)} %bitcast.79), calls=%async_computation.9 | async-start | bytes 3407872
  195.9 17.3 %slice-start = ((s8[8257536]{0:T(1024)(128)(4,1)}), s8[4194304]{0:T(1024)(128)(4,1)S(1)}, s32[]{:S(2)}) async-start(s8[8257536]{0:T(1024)(128)(4,1)} %bitcast.77), calls=%async_computation.6 | async-start | bytes 8388608
  231.0 344.4 %reduce-scatter.4.cloned.1.call-start = ((), (), s32[]{:S(2)}) async-start(), calls=%async_computation.4 | async-start | bytes 17031168 | tf_op jit(solution)/shard_map/reduce_scatter | solution.py:274
  250.9 28.3 %copy-start.3 = (bf16[640,768]{0,1:T(8,128)(2,1)S(1)}, bf16[640,768]{0,1:T(8,128)(2,1)}, u32[]{:S(2)}) copy-start(bf16[640,768]{0,1:T(8,128)(2,1)} %copy-done.2) | copy-start | bytes 2949124
  287.0 14.8 %copy-start.10 = (bf16[12,64,640]{2,1,0:T(8,128)(2,1)}, bf16[12,64,640]{2,1,0:T(8,128)(2,1)S(1)}, u32[]{:S(2)}) copy-start(bf16[12,64,640]{2,1,0:T(8,128)(2,1)S(1)} %get-tuple-element.151) | copy-start | bytes 2949124
  332.4 54.4 %copy-start.7 = (f32[640,768]{1,0:T(8,128)S(1)}, f32[640,768]{1,0:T(8,128)}, u32[]{:S(2)}) copy-start(f32[640,768]{1,0:T(8,128)} %copy-done.6) | copy-start | bytes 5898244
  332.5 54.4 %copy-start.11 = (bf16[12,64,640]{2,1,0:T(8,128)(2,1)S(1)}, bf16[12,64,640]{2,1,0:T(8,128)(2,1)}, u32[]{:S(2)}) copy-start(bf16[12,64,640]{2,1,0:T(8,128)(2,1)} %copy-done.10) | copy-start | bytes 2949124
  579.1 54.1 %copy-start.25 = (f32[12,24]{1,0:T(8,128)S(1)}, f32[12,24]{1,0:T(8,128)}, u32[]{:S(2)}) copy-start(f32[12,24]{1,0:T(8,128)} %param.22) | copy-start | bytes 3460
  579.1 54.1 %copy-start.26 = (f32[12,24]{1,0:T(8,128)S(1)}, f32[12,24]{1,0:T(8,128)}, u32[]{:S(2)}) copy-start(f32[12,24]{1,0:T(8,128)} %param.28) | copy-start | bytes 3460
  579.1 55.6 %copy-start.14 = (f32[120,768]{1,0:T(8,128)S(1)}, f32[120,768]{1,0:T(8,128)}, u32[]{:S(2)}) copy-start(f32[120,768]{1,0:T(8,128)} %param.21) | copy-start | bytes 1105924
  579.1 55.6 %copy-start.15 = (f32[120,768]{1,0:T(8,128)S(1)}, f32[120,768]{1,0:T(8,128)}, u32[]{:S(2)}) copy-start(f32[120,768]{1,0:T(8,128)} %reduce-scatter.6.cloned.1.call-done) | copy-start | bytes 1105924
  579.2 55.6 %copy-start.22 = (f32[120,768]{1,0:T(8,128)S(1)}, f32[120,768]{1,0:T(8,128)}, u32[]{:S(2)}) copy-start(f32[120,768]{1,0:T(8,128)} %param.27) | copy-start | bytes 1105924
  579.2 55.5 %copy-start.23 = (f32[120,768]{1,0:T(8,128)S(1)}, f32[120,768]{1,0:T(8,128)}, u32[]{:S(2)}) copy-start(f32[120,768]{1,0:T(8,128)} %param.24) | copy-start | bytes 1105924
  579.2 56.8 %copy-start.12 = (f32[24,5376]{1,0:T(8,128)S(1)}, f32[24,5376]{1,0:T(8,128)}, u32[]{:S(2)}) copy-start(f32[24,5376]{1,0:T(8,128)} %param.20) | copy-start | bytes 1548292
  579.2 56.8 %copy-start.13 = (f32[24,5376]{1,0:T(8,128)S(1)}, f32[24,5376]{1,0:T(8,128)}, u32[]{:S(2)}) copy-start(f32[24,5376]{1,0:T(8,128)} %reduce-scatter.4.cloned.1.call-done) | copy-start | bytes 1548292
  579.2 56.8 %copy-start.20 = (f32[24,5376]{1,0:T(8,128)S(1)}, f32[24,5376]{1,0:T(8,128)}, u32[]{:S(2)}) copy-start(f32[24,5376]{1,0:T(8,128)} %param.26) | copy-start | bytes 1548292
  579.2 56.8 %copy-start.21 = (f32[24,5376]{1,0:T(8,128)S(1)}, f32[24,5376]{1,0:T(8,128)}, u32[]{:S(2)}) copy-start(f32[24,5376]{1,0:T(8,128)} %param.23) | copy-start | bytes 1548292
  (15 other events, 110.7 us)
Sparse Core Ops, SparseCore 0:
  11.6 80.3 all-gather.3
  95.5 66.3 all-gather.5
  231.2 146.7 reduce-scatter.5
  385.2 190.0 reduce-scatter.3
where the time goes:
time: 656 us; the launch traced here: 646 us
  waiting for transfers between devices  195 us (30%)
  matrix products  154 us (23%)
  blocking collectives  151 us (23%)
  local copies, waits for them, and re-layouts  75.2 us (11%)
  other arithmetic  51.4 us (8%)
  between operations  19.3 us (3%)
    reduce_scatter x1, waiting for transfers between devices, body(): lax.psum_scatter(full_in, ('dp', 'fsdp'), scatter_dimension=0, tiled=True)  181 us
    all_gather x1, blocking collectives, body(): lax.all_gather(low_small, ('dp', 'fsdp'), axis=1, tiled=True)  71.6 us
    unnamed x74, local copies, waits for them, and re-layouts  61.7 us
    unnamed x1, blocking collectives  39.7 us
    psum x1, blocking collectives, body(): total_squares = lax.psum(local_squares, ('dp', 'fsdp'))  39.3 us
    sub x1, matrix products, backward(): grad_probs - jnp.sum(attn_probs * grad_probs, axis=2, keepdims=True)  28.2 us
    dot_general x1, matrix products, forward(): jnp.dot(hidden_low, weight_in[:, 3 * model_width:], preferred_element_typ...  23.9 us
    broadcast_in_dim x1, other arithmetic, body(): scores.astype(jnp.bfloat16)[None]  17.7 us
  transfers between devices with their start and end apart: 4, of which 2 were waited for; matrix products, arithmetic and copies ran while one was open for 29% of the time, Pallas kernels for 0%

commit v1 on v0

--- a/solution.py
+++ b/solution.py
@@ -14,6 +14,18 @@
 rate_vector = 0.25
 decay_matrix = 0.01
 masked_fill = -1e30
+
+
+def doubled_up(value, axis, dim):
+    ways, here = (lax.axis_size(axis), lax.axis_index(axis))
+    grown, reach = (value, 1)
+    while reach < ways:
+        theirs = lax.ppermute(grown, axis, [(d, d ^ reach) for d in range(ways)])
+        mine_first = jnp.concatenate([grown, theirs], axis=dim)
+        theirs_first = jnp.concatenate([theirs, grown], axis=dim)
+        grown = jnp.where(here & reach == 0, mine_first, theirs_first)
+        reach = 2 * reach
+    return grown
 
 
 def gelu_exact(upward):
@@ -254,7 +266,7 @@
     low_small = vectors.astype(jnp.bfloat16)
     gathered = (
         lax.all_gather(low_in, ("dp", "fsdp"), axis=0, tiled=True),
-        lax.all_gather(low_out, ("dp", "fsdp"), axis=0, tiled=True),
+        doubled_up(low_out, ("dp", "fsdp"), 0),
         lax.all_gather(low_small, ("dp", "fsdp"), axis=1, tiled=True),
     )
     segments = segment_ids[0]

time: 656 us -> 751 us (1.14)
  waiting for transfers between devices: 195 us -> 243 us
  matrix products: 154 us -> 182 us
  other arithmetic: 51.4 us -> 63.2 us
  starting transfers between devices: 0.16 us -> 9.99 us
    ppermute x0 -> x5, waiting for transfers between devices: none -> 60.6 us  [doubled_up(): theirs = lax.ppermute(grown, axis, [(d, d ^ reach) for d in range(ways)])]
    dot_general x1 -> x2, matrix products: 3.45 us -> 29.9 us  [forward(): jnp.dot(activated, weight_out[model_width:], preferred_element_type=jnp.f...]
    all_gather x1, waiting for transfers between devices: 14.3 us -> 0.01 us  [body(): lax.all_gather(low_out, ('dp', 'fsdp'), axis=0, tiled=True)]
    select_n x0 -> x5, other arithmetic: none -> 12 us  [doubled_up(): grown = jnp.where(here & reach == 0, mine_first, theirs_first)]
    ppermute x0 -> x5, starting transfers between devices: none -> 9.83 us  [doubled_up(): theirs = lax.ppermute(grown, axis, [(d, d ^ reach) for d in range(ways)])]
    unnamed x74 -> x104, local copies, waits for them, and re-layouts: 61.7 us -> 63.2 us
  transfers between devices with their start and end apart: 4 -> 9, of which waited for: 2 -> 5; matrix products, arithmetic and copies ran while one was open for 29% -> 31% of each run, Pallas kernels for 0% -> 0%
where the time goes in v1:
time: 751 us; the launch traced here: 740 us
  waiting for transfers between devices  243 us (32%)
  matrix products  182 us (24%)
  blocking collectives  145 us (19%)
  local copies, waits for them, and re-layouts  77.3 us (10%)
  other arithmetic  63.2 us (8%)
  between operations  19.5 us (3%)
  starting transfers between devices  9.99 us (1%)
    reduce_scatter x1, waiting for transfers between devices, body(): lax.psum_scatter(full_in, ('dp', 'fsdp'), scatter_dimension=0, tiled=True)  182 us
    all_gather x1, blocking collectives, body(): lax.all_gather(low_small, ('dp', 'fsdp'), axis=1, tiled=True)  68.5 us
    unnamed x104, local copies, waits for them, and re-layouts  63.2 us
    ppermute x5, waiting for transfers between devices, doubled_up(): theirs = lax.ppermute(grown, axis, [(d, d ^ reach) for d in range(ways)])  60.6 us
    psum x1, blocking collectives, body(): total_squares = lax.psum(local_squares, ('dp', 'fsdp'))  39.2 us
    unnamed x1, blocking collectives  37.8 us
    dot_general x2, matrix products, forward(): jnp.dot(activated, weight_out[model_width:], preferred_element_type=jnp.f...  29.9 us
    sub x1, matrix products, backward(): grad_probs - jnp.sum(attn_probs * grad_probs, axis=2, keepdims=True)  28.1 us
  transfers between devices with their start and end apart: 9, of which 5 were waited for; matrix products, arithmetic and copies ran while one was open for 31% of the time, Pallas kernels for 0%

profile of v1, /device:TPU:0, one launch (start us, length us, event | category | flops | bytes accessed | tf_op | source)
XLA Modules:
  0.0 740.4 jit_solution(7509389229638593081)
XLA Ops:
  19.7 10.2 %collective-permute-done.1 = bf16[240,768]{1,0:T(8,128)(2,1)S(1)} collective-permute-done((bf16[240,768]{1,0:T(8,128)(2,1)S(1)}, bf16[240,768]{1,0:T(8,128)(2,1)S(1)}, u32[]{:S(2)}, u32[]{:S(2)}) %collective-permute-start.1) | collective-permute-done | bytes 368672 | tf_op jit(solution)/shard_map/ppermute | solution.py:23
  33.3 43.3 %collective-permute-done.2 = bf16[480,768]{1,0:T(8,128)(2,1)S(1)} collective-permute-done((bf16[480,768]{1,0:T(8,128)(2,1)S(1)}, bf16[480,768]{1,0:T(8,128)(2,1)S(1)}, u32[]{:S(2)}, u32[]{:S(2)}) %collective-permute-start.2) | collective-permute-done | bytes 737312 | tf_op jit(solution)/shard_map/ppermute | solution.py:23
  86.6 68.5 %all-gather = bf16[32,24,12]{1,2,0:T(8,128)(2,1)S(1)} all-gather(bf16[1,24,12]{1,2,0:T(8,128)(2,1)S(1)} %convert_bitcast_fusion.1), channel_id=1, replica_groups=mesh['dp'=4,'fsdp'=8] {'dp','fsdp'}, dimensions={0}, use_global_device_ids=true | all-gather | bytes 19008 | tf_op jit(solution)/shard_map/all_gather | solution.py:270
  155.5 13.8 %copy.85 = bf16[1,12,640,640]{2,3,1,0:T(8,128)(2,1)} copy(bf16[1,12,640,640]{3,2,1,0:T(8,128)(2,1)} %param.16) | data formatting | bytes 19660800 | tf_op args[1]
  170.2 7.1 maximum_select_fusion
  186.8 12.2 %select_reduce_fusion = (f32[12,640]{1,0:T(8,128)S(1)}, f32[12,640,640]{1,2,0:T(8,128)}) fusion(pred[640,640]{0,1:T(8,128)(4,1)S(1)} %broadcast_compare_fusion, bf16[1,12,640,640]{2,3,1,0:T(8,128)(2,1)} %copy.85, bf16[640,12,64]{0,2,1:T(8,128)(2,1)S(1)} %bitcast.64, bf16[640,12,64]{0,2,1:T(8,128)(2,1)S(1)} %bitcast.62), kind=kOutput, calls=%fused_computation.11 | convolution fusion | flops 653713920 | bytes 31897600 | tf_op jit(solution)/shard_map/qhd,khd->hqk/dot_general | solution.py:66
  199.0 17.6 %convert_bitcast_fusion = (bf16[1,12,640,640]{2,3,1,0:T(8,128)(2,1)}, f32[12,640]{1,0:T(8,128)S(1)}) fusion(f32[12,640,640]{1,2,0:T(8,128)} %get-tuple-element.143, f32[12,640]{1,0:T(8,128)S(1)} %get-tuple-element.142, pred[640,640]{0,1:T(8,128)(4,1)S(1)} %broadcast_compare_fusion), kind=kLoop, calls=%fused_computation.19 | loop fusion | flops 19653120 | bytes 29962240 | tf_op jit(solution)/shard_map/broadcast_in_dim | solution.py:311
  216.6 9.7 %fusion.106 = bf16[12,64,640]{2,1,0:T(8,128)(2,1)S(1)} fusion(bf16[640,12,64]{0,2,1:T(8,128)(2,1)S(1)} %bitcast.68, f32[12,640,640]{1,2,0:T(8,128)} %get-tuple-element.143, f32[12,640]{1,0:T(8,128)S(1)} %get-tuple-element.138, f32[12,640]{1,0:T(8,128)S(1)} %get-tuple-element.142, pred[640,640]{0,1:T(8,128)(4,1)S(1)} %broadcast_compare_fusion), kind=kOutput, calls=%fused_computation.153 | convolution fusion | flops 649297920 | bytes 22097920 | tf_op jit(solution)/shard_map/hqk,khd->qhd/dot_general | solution.py:78
  230.4 26.5 %fusion.179 = (f32[640]{0:T(1024)S(1)}, f32[640,768]{1,0:T(8,128)S(1)}) fusion(f32[768]{0:T(1024)S(1)} %get-tuple-element.110, bf16[3840,768]{1,0:T(8,128)(2,1)} %maximum_select_fusion, f32[3072]{0:T(1024)S(1)} %add.249, bf16[768,5376]{1,0:T(8,128)(2,1)} %all-gather.4.cloned.1.call-done, f32[640,768]{1,0:T(8,128)} %copy-done.19, ...), kind=kOutput, calls=%fused_computation.254 | convolution fusion | flops 6175456768 | bytes 15387136 | tf_op jit(solution)/shard_map/dot_general | solution.py:96
  261.5 23.7 %multiply_convert_fusion = (bf16[640,3072]{1,0:T(8,128)(2,1)S(1)}, f32[640,3072]{1,0:T(8,128)}, f32[640,3072]{1,0:T(8,128)}) fusion(f32[3072]{0:T(1024)S(1)} %add.249, bf16[768,5376]{1,0:T(8,128)(2,1)} %all-gather.4.cloned.1.call-done, f32[640,768]{1,0:T(8,128)S(1)} %get-tuple-element.145, f32[640]{0:T(1024)S(1)} %add_rsqrt_fusion.1, ...), kind=kOutput, calls=%fused_computation.31 | convolution fusion | flops 3152117760 | bytes 26369024 | tf_op jit(solution)/shard_map/dot_general | solution.py:91
  292.5 6.8 fusion.130
  299.2 10.4 %convert_reduce_fusion = (f32[3072]{0:T(1024)S(1)}, bf16[640,3072]{1,0:T(8,128)(2,1)S(1)}) fusion(f32[640,3072]{1,0:T(8,128)} %get-tuple-element.136, bf16[3840,768]{1,0:T(8,128)(2,1)} %all-gather.6.cloned.1.call-done, f32[640,768]{1,0:T(8,128)S(1)} %get-tuple-element.132, f32[640,3072]{1,0:T(8,128)} %get-tuple-element.146, f32[3072]{0:T(1024)S(1)} %add.249), kind=kOutput, calls=%fused_computation.29 | convolution fusion | flops 3053810688 | bytes 26370048 | tf_op jit(solution)/shard_map/td,fd->tf/dot_general | solution.py:145
  318.0 9.5 %pad_maximum_fusion.1 = f32[3840,768]{1,0:T(8,128)} fusion(f32[3072,768]{1,0:T(8,128)} %fusion.130, f32[768,768]{1,0:T(8,128)} %fusion.127), kind=kLoop, calls=%fused_computation.13 | loop fusion | flops 2949120 | bytes 23592960 | tf_op jit(solution)/shard_map/concatenate | solution.py:228
  327.5 14.6 %copy.88 = bf16[1,12,640,640]{2,3,1,0:T(8,128)(2,1)} copy(bf16[1,12,640,640]{3,2,1,0:T(8,128)(2,1)} %param.19) | data formatting | bytes 19660800 | tf_op args[4]
  346.5 28.1 %fusion.1 = bf16[12,640,640]{1,2,0:T(8,128)(2,1)} fusion(f32[12,640,640]{1,2,0:T(8,128)} %get-tuple-element.143, bf16[1,12,640,640]{2,3,1,0:T(8,128)(2,1)} %copy.88, f32[12,640]{1,0:T(8,128)S(1)} %log_add_fusion, pred[640,640]{0,1:T(8,128)(4,1)S(1)} %copy-done.14, bf16[640,12,64]{0,2,1:T(8,128)(2,1)} %bitcast.75, bf16[640,12,64]{0,2,1:T(8,128)(2,1)} %bitcast.69), kind=kOutput, calls=%fused_computation.2 | convolution fusion | flops 1307451520 | bytes 41728000 | tf_op jit(solution)/shard_map/sub | solution.py:176
  385.7 11.5 %convert_reduce_fusion.4 = (f32[12,64]{1,0:T(8,128)S(1)}, bf16[12,64,640]{2,1,0:T(8,128)(2,1)S(1)}) fusion(bf16[640,12,64]{0,2,1:T(8,128)(2,1)S(1)} %bitcast.76, f32[12,640,640]{1,2,0:T(8,128)} %get-tuple-element.143, f32[12,640]{1,0:T(8,128)S(1)} %log_add_fusion, pred[640,640]{0,1:T(8,128)(4,1)S(1)} %copy-done.14), kind=kOutput, calls=%fused_computation.129 | convolution fusion | flops 645364992 | bytes 22070272 | tf_op jit(solution)/shard_map/hqk,qhd->khd/dot_general | solution.py:196
  398.2 7.9 %convolution_bitcast_fusion = f32[768,2304]{0,1:T(8,128)} fusion(bf16[640,768]{1,0:T(8,128)(2,1)S(1)} %copy-done.44, bf16[640,768]{0,1:T(8,128)(2,1)S(1)} %bitcast.83, bf16[640,768]{0,1:T(8,128)(2,1)S(1)} %bitcast.73, bf16[640,768]{0,1:T(8,128)(2,1)S(1)} %bitcast.66), kind=kOutput, calls=%fused_computation.61 | convolution fusion | flops 2273771520 | bytes 11010048 | tf_op jit(solution)/shard_map/td,tc->dc/dot_general | solution.py:206
  406.2 8.2 %copy.92 = f32[768,2304]{1,0:T(8,128)} copy(f32[768,2304]{0,1:T(8,128)} %convolution_bitcast_fusion) | data formatting | bytes 14155776 | tf_op jit(solution)/shard_map/td,tc->dc/dot_general | solution.py:206
  414.4 6.5 fusion.165
  427.8 14.3 %copy.94 = bf16[1,12,640,640]{3,2,1,0:T(8,128)(2,1)} copy(bf16[1,12,640,640]{2,3,1,0:T(8,128)(2,1)} %bitcast.61) | data formatting | bytes 19660800
  442.2 37.8 %all-reduce = f32[12,768]{1,0:T(8,128)S(1)} all-reduce(f32[12,768]{1,0:T(8,128)S(1)} %concatenate.55), channel_id=4, replica_groups=mesh['dp'=4,'fsdp'=8] {'dp','fsdp'}, use_global_device_ids=true, to_apply=%region_28.29.clone | all-reduce | flops 9216 | bytes 73728
  488.5 181.9 %reduce-scatter.4.cloned.1.call-done = f32[24,5376]{1,0:T(8,128)} async-done(((f32[768,5376]{1,0:T(8,128)}), f32[24,5376]{1,0:T(8,128)}) %reduce-scatter.4.cloned.1.call-update) | async-done | bytes 516112 | tf_op jit(solution)/shard_map/reduce_scatter | solution.py:286
  674.2 13.9 %copy.93 = bf16[1,12,640,640]{3,2,1,0:T(8,128)(2,1)} copy(bf16[1,12,640,640]{2,3,1,0:T(8,128)(2,1)} %get-tuple-element.137) | data formatting | bytes 19660800
  688.2 39.2 %psum.7 = f32[]{:T(128)} all-reduce(f32[]{:T(128)S(6)} %add.273), channel_id=1, replica_groups=mesh['dp'=4,'fsdp'=8] {'dp','fsdp'}, use_global_device_ids=true, to_apply=%region_30.31 | all-reduce | flops 1 | bytes 8 | tf_op jit(solution)/shard_map/psum | solution.py:295
  (188 shorter events, 97.6 us)
Async XLA Ops:
  7.2 79.4 %copy-start.38 = (f32[12,24]{1,0:T(8,128)S(1)}, f32[12,24]{1,0:T(8,128)}, u32[]{:S(2)}) copy-start(f32[12,24]{1,0:T(8,128)} %param.22) | copy-start | bytes 3460
  7.2 148.3 %copy-start.42 = (s32[1,640]{1,0:T(1,128)S(1)}, s32[1,640]{1,0:T(1,128)}, u32[]{:S(2)}) copy-start(s32[1,640]{1,0:T(1,128)} %param.17) | copy-start | bytes 7684
  7.2 170.1 %all-gather.4.cloned.1.call-start = ((), (), s32[]{:S(2)}) async-start(), calls=%async_computation.2 | async-start | bytes 8515584 | tf_op jit(solution)/shard_map/all_gather | solution.py:268
  9.0 249.1 %all-gather.6.cloned.1.call-start = ((), (), s32[]{:S(2)}) async-start(), calls=%async_computation.3 | async-start | bytes 6082560 | tf_op jit(solution)/shard_map/all_gather | solution.py:278
  10.1 76.4 %copy-start.20 = (bf16[120,768]{1,0:T(8,128)(2,1)}, bf16[120,768]{1,0:T(8,128)(2,1)S(1)}, u32[]{:S(2)}) copy-start(bf16[120,768]{1,0:T(8,128)(2,1)S(1)} %convert_element_type.158) | copy-start | bytes 552964
  10.1 7.6 %collective-permute-start = (bf16[120,768]{1,0:T(8,128)(2,1)S(1)}, bf16[120,768]{1,0:T(8,128)(2,1)S(1)}, u32[]{:S(2)}, u32[]{:S(2)}) collective-permute-start(bf16[120,768]{1,0:T(8,128)(2,1)S(1)} %convert_element_type.158), channel_id=1, source_target_pairs={{0,1},{1,0},{2,3},{3,2},{4,5},{5,4},{6,7},{7,6},{8,9},{9,8},{10,11... | collective-permute-start | bytes 552968 | tf_op jit(solution)/shard_map/ppermute | solution.py:23
  17.8 12.1 %collective-permute-start.1 = (bf16[240,768]{1,0:T(8,128)(2,1)S(1)}, bf16[240,768]{1,0:T(8,128)(2,1)S(1)}, u32[]{:S(2)}, u32[]{:S(2)}) collective-permute-start(bf16[240,768]{1,0:T(8,128)(2,1)S(1)} %maximum_select_fusion.4), channel_id=1, source_target_pairs={{0,2},{1,3},{2,0},{3,1},{4,6},{5,7},{6,4},{7,5},{8,10},{9,11},{10,... | collective-permute-start | bytes 1105928 | tf_op jit(solution)/shard_map/ppermute | solution.py:23
  30.2 46.4 %collective-permute-start.2 = (bf16[480,768]{1,0:T(8,128)(2,1)S(1)}, bf16[480,768]{1,0:T(8,128)(2,1)S(1)}, u32[]{:S(2)}, u32[]{:S(2)}) collective-permute-start(bf16[480,768]{1,0:T(8,128)(2,1)S(1)} %maximum_select_fusion.3), channel_id=1, source_target_pairs={{0,4},{1,5},{2,6},{3,7},{4,0},{5,1},{6,2},{7,3},{8,12},{9,13},{10,... | collective-permute-start | bytes 2211848 | tf_op jit(solution)/shard_map/ppermute | solution.py:23
  77.3 3.5 collective-permute-start.3
  84.7 85.6 %collective-permute-start.4 = (bf16[1920,768]{1,0:T(8,128)(2,1)S(1)}, bf16[1920,768]{1,0:T(8,128)(2,1)}, u32[]{:S(2)}, u32[]{:S(2)}) collective-permute-start(bf16[1920,768]{1,0:T(8,128)(2,1)S(1)} %maximum_select_fusion.1), channel_id=1, source_target_pairs={{0,16},{1,17},{2,18},{3,19},{4,20},{5,21},{6,22},{7,23},{8,24},{9,... | collective-permute-start | bytes 8847368 | tf_op jit(solution)/shard_map/ppermute | solution.py:23
  86.5 400.2 %reduce-scatter.6.cloned.1.call-start = ((), (), s32[]{:S(2)}) async-start(), calls=%async_computation.5 | async-start | bytes 12165120 | tf_op jit(solution)/shard_map/reduce_scatter | solution.py:287
  327.5 342.9 %reduce-scatter.4.cloned.1.call-start = ((), (), s32[]{:S(2)}) async-start(), calls=%async_computation.4 | async-start | bytes 17031168 | tf_op jit(solution)/shard_map/reduce_scatter | solution.py:286
  427.8 52.9 %copy-start.9 = (f32[640,768]{1,0:T(8,128)S(1)}, f32[640,768]{1,0:T(8,128)}, u32[]{:S(2)}) copy-start(f32[640,768]{1,0:T(8,128)} %copy-done.8) | copy-start | bytes 5898244
  427.8 52.9 %copy-start.16 = (bf16[12,64,640]{2,1,0:T(8,128)(2,1)S(1)}, bf16[12,64,640]{2,1,0:T(8,128)(2,1)}, u32[]{:S(2)}) copy-start(bf16[12,64,640]{2,1,0:T(8,128)(2,1)} %copy-done.15) | copy-start | bytes 2949124
  674.1 54.0 %copy-start.39 = (f32[12,24]{1,0:T(8,128)S(1)}, f32[12,24]{1,0:T(8,128)}, u32[]{:S(2)}) copy-start(f32[12,24]{1,0:T(8,128)} %param.22) | copy-start | bytes 3460
  674.1 54.0 %copy-start.41 = (f32[12,24]{1,0:T(8,128)S(1)}, f32[12,24]{1,0:T(8,128)}, u32[]{:S(2)}) copy-start(f32[12,24]{1,0:T(8,128)} %param.28) | copy-start | bytes 3460
  674.1 55.4 %copy-start.21 = (f32[120,768]{1,0:T(8,128)S(1)}, f32[120,768]{1,0:T(8,128)}, u32[]{:S(2)}) copy-start(f32[120,768]{1,0:T(8,128)} %param.21) | copy-start | bytes 1105924
  674.1 55.4 %copy-start.22 = (f32[120,768]{1,0:T(8,128)S(1)}, f32[120,768]{1,0:T(8,128)}, u32[]{:S(2)}) copy-start(f32[120,768]{1,0:T(8,128)} %reduce-scatter.6.cloned.1.call-done) | copy-start | bytes 1105924
  674.2 55.4 %copy-start.32 = (f32[120,768]{1,0:T(8,128)S(1)}, f32[120,768]{1,0:T(8,128)}, u32[]{:S(2)}) copy-start(f32[120,768]{1,0:T(8,128)} %param.27) | copy-start | bytes 1105924
  674.2 55.4 %copy-start.33 = (f32[120,768]{1,0:T(8,128)S(1)}, f32[120,768]{1,0:T(8,128)}, u32[]{:S(2)}) copy-start(f32[120,768]{1,0:T(8,128)} %param.24) | copy-start | bytes 1105924
  674.2 56.7 %copy-start.17 = (f32[24,5376]{1,0:T(8,128)S(1)}, f32[24,5376]{1,0:T(8,128)}, u32[]{:S(2)}) copy-start(f32[24,5376]{1,0:T(8,128)} %param.20) | copy-start | bytes 1548292
  674.2 56.6 %copy-start.18 = (f32[24,5376]{1,0:T(8,128)S(1)}, f32[24,5376]{1,0:T(8,128)}, u32[]{:S(2)}) copy-start(f32[24,5376]{1,0:T(8,128)} %reduce-scatter.4.cloned.1.call-done) | copy-start | bytes 1548292
  674.2 56.6 %copy-start.28 = (f32[24,5376]{1,0:T(8,128)S(1)}, f32[24,5376]{1,0:T(8,128)}, u32[]{:S(2)}) copy-start(f32[24,5376]{1,0:T(8,128)} %param.26) | copy-start | bytes 1548292
  674.2 56.6 %copy-start.29 = (f32[24,5376]{1,0:T(8,128)S(1)}, f32[24,5376]{1,0:T(8,128)}, u32[]{:S(2)}) copy-start(f32[24,5376]{1,0:T(8,128)} %param.23) | copy-start | bytes 1548292
  (35 other events, 434.6 us)
Sparse Core Ops, SparseCore 0:
  11.6 112.4 all-gather.3
  127.7 68.6 all-gather.5
  327.6 145.2 reduce-scatter.5
  480.2 190.0 reduce-scatter.3
